TPU v7x, 32 devices: a whole 2x2x4 slice. The times are simulated.
32 devices in a mesh: fsdp: 8 (over y, x, core), tp: 4 (over z).
Axes of the slice: x: 2, y: 2, z: 4, core: 2. Of those that a mesh axis runs over, the one named last changes fastest.
Arguments:
- tokens: bfloat16 [8192, 2048], P(('fsdp', 'tp')), may hold values from -6 to 6
- norm1_gain: float32 [2048], replicated, may hold values from 0.25 to 1.75
- norm1_shift: float32 [2048], replicated, may hold values from -1 to 1
- w_query: bfloat16 [2048, 2048], P('fsdp', 'tp'), may hold values from -0.125 to 0.125
- b_query: float32 [2048], P('tp'), may hold values from -1 to 1
- w_key: bfloat16 [2048, 2048], P('fsdp', 'tp'), may hold values from -0.125 to 0.125
- w_value: bfloat16 [2048, 2048], P('fsdp', 'tp'), may hold values from -0.125 to 0.125
- b_value: float32 [2048], P('tp'), may hold values from -1 to 1
- w_out: bfloat16 [2048, 2048], P('fsdp', 'tp'), may hold values from -0.5 to 0.5
- b_out: float32 [2048], replicated, may hold values from -1 to 1
- norm2_gain: float32 [2048], replicated, may hold values from 0.25 to 1.75
- norm2_shift: float32 [2048], replicated, may hold values from -1 to 1
- w_up: bfloat16 [2048, 8192], P('fsdp', 'tp'), may hold values from -0.125 to 0.125
- b_up: float32 [8192], P('tp'), may hold values from -1 to 1
- w_down: bfloat16 [2048, 8192], P('fsdp', 'tp'), may hold values from -0.09375 to 0.09375
- b_down: float32 [2048], replicated, may hold values from -1 to 1
- teacher: bfloat16 [8192, 2048], P(('fsdp', 'tp')), may hold values from -6 to 6
- valid_mask: int32 [8192], P(('fsdp', 'tp')), may hold values from 0 to 1, as said below
- parents: int32 [8, 8], P('fsdp'), may hold values from -1 to 6, as said below
- summary: int32 [8, 8, 12], P('fsdp'), may hold values from 0 to 127, as said below
Outputs:
- output_states: bfloat16 [8192, 2048], P(('fsdp', 'tp'))
- mean_loss: float32 [], replicated
- grad_tokens: float32 [8192, 2048], P(('fsdp', 'tp'))
- grad_norm1_gain: float32 [2048], replicated
- grad_norm1_shift: float32 [2048], replicated
- grad_w_query: float32 [2048, 2048], P('fsdp', 'tp')
- grad_b_query: float32 [2048], P('tp')
- grad_w_key: float32 [2048, 2048], P('fsdp', 'tp')
- grad_w_value: float32 [2048, 2048], P('fsdp', 'tp')
- grad_b_value: float32 [2048], P('tp')
- grad_w_out: float32 [2048, 2048], P('fsdp', 'tp')
- grad_b_out: float32 [2048], replicated
- grad_norm2_gain: float32 [2048], replicated
- grad_norm2_shift: float32 [2048], replicated
- grad_w_up: float32 [2048, 8192], P('fsdp', 'tp')
- grad_b_up: float32 [8192], P('tp')
- grad_w_down: float32 [2048, 8192], P('fsdp', 'tp')
- grad_b_down: float32 [2048], replicated
Inputs may be any that keep to these rules, and one draw needn't show every extreme that they name: valid_mask is 1 at the first token of every tree. parents[f, 0] is -1 and 0 <= parents[f, s] < s for every later segment s; the last segment of every tree has the segment before it as parent. `summary`: the 12 offsets of one segment are distinct.
All inputs are finite; a program needn't handle non-finite values.
Results may differ from a plain program's by a relative error of at most 0.019.
Values may be sent and summed in bfloat16 or wider, within the bound.
No kernel may reach another device: no remote copies, remote signals or barrier semaphores. Data moves between devices by JAX's collectives and lax.ppermute only.
A program may use at most 192 MiB of HBM per device.

v0:
```python
import jax
import jax.numpy as jnp
from jax import lax
from jax.sharding import PartitionSpec as P

HD = 64
EPSILON = 1e-05
MASKED_SCORE = -1e30


def layer_norm(vectors, norm_gain, norm_shift):
    centre = jnp.mean(vectors, axis=-1, keepdims=True)
    centred = vectors - centre
    spread = jnp.mean(centred * centred, axis=-1, keepdims=True)
    return centred * lax.rsqrt(spread + EPSILON) * norm_gain + norm_shift


def ancestors(parent_row):
    segments = parent_row.shape[0]
    columns = jnp.arange(segments, dtype=jnp.int32)

    def follow(sweep, state_pair):
        ancestry, current = state_pair
        matches = current[:, None] == columns[None, :]
        ancestry = jnp.maximum(ancestry, matches.astype(jnp.float32))
        following = jnp.sum(jnp.where(matches, parent_row[None, :], 0), axis=1)
        current = jnp.where(current >= 0, following, -1)
        return (ancestry, current)

    start_table = jnp.zeros((segments, segments), jnp.float32)
    ancestry, finished = lax.fori_loop(0, segments, follow, (start_table, parent_row))
    return ancestry


def tree_tables(parent_row, summary_rows, length):
    segments = parent_row.shape[0]
    seg_length = length // segments
    ancestry = ancestors(parent_row)
    offsets = jnp.arange(seg_length, dtype=jnp.int32)
    marked = jnp.max(
        (summary_rows[:, :, None] == offsets[None, None, :]).astype(jnp.float32), axis=1
    ).reshape(length)
    key_segment = jnp.arange(length, dtype=jnp.int32) // seg_length
    key_onehot = (key_segment[:, None] == jnp.arange(segments, dtype=jnp.int32)[None, :]).astype(
        jnp.float32
    )
    return (ancestry, marked, key_segment, key_onehot, seg_length)


def block_mask(tables, start_row, block_rows):
    ancestry, marked, key_segment, key_onehot, seg_length = tables
    query_position = start_row + jnp.arange(block_rows, dtype=jnp.int32)
    query_segment = query_position // seg_length
    query_onehot = (
        query_segment[:, None] == jnp.arange(ancestry.shape[0], dtype=jnp.int32)[None, :]
    ).astype(jnp.float32)
    reached = jnp.dot(jnp.dot(query_onehot, ancestry, precision=None), key_onehot.T, precision=None)
    key_position = jnp.arange(marked.shape[0], dtype=jnp.int32)
    same_segment = (query_segment[:, None] == key_segment[None, :]) & (
        key_position[None, :] <= query_position[:, None]
    )
    return same_segment | (reached > 0.5) & (marked[None, :] > 0.5)


def contract(left_side, right_side, left_dim, right_dim):
    return lax.dot_general(
        left_side,
        right_side,
        (((left_dim,), (right_dim,)), ((), ())),
        preferred_element_type=jnp.float32,
    )


def attend_forward(queries, key_states, value_states, tables):
    length = queries.shape[0]
    head_count = queries.shape[1] // HD
    block_rows = min(512, length)
    query_heads = queries.reshape(length, head_count, HD)
    key_heads = key_states.reshape(length, head_count, HD)
    value_heads = value_states.reshape(length, head_count, HD)

    def one_block(start_row):
        query_block = lax.dynamic_slice_in_dim(query_heads, start_row, block_rows, 0)
        scores = jnp.einsum(
            "qhd,khd->hqk", query_block, key_heads, preferred_element_type=jnp.float32
        )
        allowed = block_mask(tables, start_row, block_rows)
        scores = jnp.where(allowed[None], scores, MASKED_SCORE)
        highest = jnp.max(scores, axis=-1, keepdims=True)
        exp_scores = jnp.exp(scores - highest)
        totals = jnp.sum(exp_scores, axis=-1, keepdims=True)
        shares = (exp_scores / totals).astype(jnp.bfloat16)
        attended = jnp.einsum(
            "hqk,khd->qhd", shares, value_heads, preferred_element_type=jnp.float32
        )
        return (attended.astype(jnp.bfloat16), (highest + jnp.log(totals))[..., 0])

    starts = jnp.arange(length // block_rows, dtype=jnp.int32) * block_rows
    attended, log_totals = lax.map(one_block, starts)
    return (attended.reshape(length, head_count * HD), log_totals)


def attend_backward(queries, key_states, value_states, grad_attended, log_totals, tables):
    length = queries.shape[0]
    head_count = queries.shape[1] // HD
    block_rows = min(512, length)
    query_heads = queries.reshape(length, head_count, HD)
    key_heads = key_states.reshape(length, head_count, HD)
    value_heads = value_states.reshape(length, head_count, HD)
    grad_heads = grad_attended.reshape(length, head_count, HD)

    def one_block(summed, members):
        start_row, log_block = members
        key_sum, value_sum = summed
        query_block = lax.dynamic_slice_in_dim(query_heads, start_row, block_rows, 0)
        grad_block = lax.dynamic_slice_in_dim(grad_heads, start_row, block_rows, 0)
        scores = jnp.einsum(
            "qhd,khd->hqk", query_block, key_heads, preferred_element_type=jnp.float32
        )
        allowed = block_mask(tables, start_row, block_rows)
        probs = jnp.where(allowed[None], jnp.exp(scores - log_block[..., None]), 0.0)
        grad_probs = jnp.einsum(
            "qhd,khd->hqk", grad_block, value_heads, preferred_element_type=jnp.float32
        )
        inner_sum = jnp.sum(probs * grad_probs, axis=-1, keepdims=True)
        grad_scores = (probs * (grad_probs - inner_sum)).astype(jnp.bfloat16)
        grad_query = jnp.einsum(
            "hqk,khd->qhd", grad_scores, key_heads, preferred_element_type=jnp.float32
        ).astype(jnp.bfloat16)
        key_sum = key_sum + jnp.einsum(
            "hqk,qhd->khd", grad_scores, query_block, preferred_element_type=jnp.float32
        )
        value_sum = value_sum + jnp.einsum(
            "hqk,qhd->khd",
            probs.astype(jnp.bfloat16),
            grad_block,
            preferred_element_type=jnp.float32,
        )
        return ((key_sum, value_sum), grad_query)

    starts = jnp.arange(length // block_rows, dtype=jnp.int32) * block_rows
    zero_heads = jnp.zeros((length, head_count, HD), jnp.float32)
    (key_sum, value_sum), grad_queries = lax.scan(
        one_block, (zero_heads, zero_heads), (starts, log_totals)
    )
    width = head_count * HD
    return (
        grad_queries.reshape(length, width),
        key_sum.reshape(length, width).astype(jnp.bfloat16),
        value_sum.reshape(length, width).astype(jnp.bfloat16),
    )


def body(
    tokens,
    norm1_gain,
    norm1_shift,
    w_query,
    b_query,
    w_key,
    w_value,
    b_value,
    w_out,
    b_out,
    norm2_gain,
    norm2_shift,
    w_up,
    b_up,
    w_down,
    b_down,
    teacher,
    valid_mask,
    parents,
    summary,
):

    def attention_weights():
        return (
            lax.all_gather(w_query, "fsdp", axis=0, tiled=True),
            lax.all_gather(w_key, "fsdp", axis=0, tiled=True),
            lax.all_gather(w_value, "fsdp", axis=0, tiled=True),
            lax.all_gather(w_out, "fsdp", axis=0, tiled=True),
        )

    def feed_weights():
        return (
            lax.all_gather(w_up, "fsdp", axis=0, tiled=True),
            lax.all_gather(w_down, "fsdp", axis=0, tiled=True),
        )

    inputs = tokens.astype(jnp.float32)
    normed = layer_norm(inputs, norm1_gain, norm1_shift).astype(jnp.bfloat16)
    normed_all = lax.all_gather(normed, "tp", axis=0, tiled=True)
    full_query, full_key, full_value, full_out = attention_weights()
    queries = (
        (jnp.dot(normed_all, full_query, preferred_element_type=jnp.float32) + b_query) * 0.125
    ).astype(jnp.bfloat16)
    key_states = jnp.dot(normed_all, full_key, preferred_element_type=jnp.float32).astype(
        jnp.bfloat16
    )
    value_states = (
        jnp.dot(normed_all, full_value, preferred_element_type=jnp.float32) + b_value
    ).astype(jnp.bfloat16)
    tables = tree_tables(parents[0], summary[0], normed_all.shape[0])
    attended, log_totals = attend_forward(queries, key_states, value_states, tables)
    branch = lax.psum_scatter(
        contract(attended, full_out, 1, 1), "tp", scatter_dimension=0, tiled=True
    )
    hidden = inputs + branch + b_out
    normed_mid = layer_norm(hidden, norm2_gain, norm2_shift).astype(jnp.bfloat16)
    normed_mid_all = lax.all_gather(normed_mid, "tp", axis=0, tiled=True)
    full_up, full_down = feed_weights()
    active = jnp.maximum(
        jnp.dot(normed_mid_all, full_up, preferred_element_type=jnp.float32) + b_up, 0.0
    ).astype(jnp.bfloat16)
    feed_out = lax.psum_scatter(
        contract(active, full_down, 1, 1), "tp", scatter_dimension=0, tiled=True
    )
    output = hidden + feed_out + b_down
    weight_mask = valid_mask.astype(jnp.float32)
    deviation = output - teacher.astype(jnp.float32)
    valid_count, squares = lax.psum(
        (jnp.sum(weight_mask), jnp.sum(weight_mask[:, None] * deviation * deviation)),
        ("fsdp", "tp"),
    )
    mean_loss = squares / (valid_count * tokens.shape[1])
    total_tokens = tokens.shape[0] * lax.axis_size("fsdp") * lax.axis_size("tp")
    grad_output = 2.0 * total_tokens / valid_count * weight_mask[:, None] * deviation
    grad_feed_all = lax.all_gather(grad_output.astype(jnp.bfloat16), "tp", axis=0, tiled=True)
    full_up, full_down = feed_weights()
    grad_w_down = contract(grad_feed_all, active, 0, 0)
    grad_pre = jnp.where(
        active > 0, jnp.dot(grad_feed_all, full_down, preferred_element_type=jnp.float32), 0.0
    ).astype(jnp.bfloat16)
    grad_w_up = contract(normed_mid_all, grad_pre, 0, 0)
    grad_w_up, grad_w_down = (
        lax.psum_scatter(
            grad_w_up.astype(jnp.bfloat16), "fsdp", scatter_dimension=0, tiled=True
        ).astype(jnp.float32),
        lax.psum_scatter(
            grad_w_down.astype(jnp.bfloat16), "fsdp", scatter_dimension=0, tiled=True
        ).astype(jnp.float32),
    )
    grad_mid = lax.psum_scatter(
        contract(grad_pre, full_up, 1, 1), "tp", scatter_dimension=0, tiled=True
    )
    second_norm, second_pull = jax.vjp(layer_norm, hidden, norm2_gain, norm2_shift)
    grad_hidden_norm, grad_norm2_gain, grad_norm2_shift = second_pull(grad_mid)
    grad_hidden = grad_output + grad_hidden_norm
    grad_branch_all = lax.all_gather(grad_hidden.astype(jnp.bfloat16), "tp", axis=0, tiled=True)
    full_query, full_key, full_value, full_out = attention_weights()
    grad_w_out = contract(grad_branch_all, attended, 0, 0)
    grad_attended = jnp.dot(grad_branch_all, full_out, preferred_element_type=jnp.float32).astype(
        jnp.bfloat16
    )
    grad_queries, grad_keys, grad_values = attend_backward(
        queries, key_states, value_states, grad_attended, log_totals, tables
    )
    grad_pre_query = grad_queries * jnp.bfloat16(0.125)
    grad_w_query = contract(normed_all, grad_pre_query, 0, 0)
    grad_w_key = contract(normed_all, grad_keys, 0, 0)
    grad_w_value = contract(normed_all, grad_values, 0, 0)
    grad_w_query, grad_w_key, grad_w_value, grad_w_out = (
        lax.psum_scatter(grad_w_query, "fsdp", scatter_dimension=0, tiled=True),
        lax.psum_scatter(grad_w_key, "fsdp", scatter_dimension=0, tiled=True),
        lax.psum_scatter(grad_w_value, "fsdp", scatter_dimension=0, tiled=True),
        lax.psum_scatter(grad_w_out, "fsdp", scatter_dimension=0, tiled=True),
    )
    grad_normed = (
        contract(grad_pre_query, full_query, 1, 1)
        + contract(grad_keys, full_key, 1, 1)
        + contract(grad_values, full_value, 1, 1)
    )
    grad_normed = lax.psum_scatter(grad_normed, "tp", scatter_dimension=0, tiled=True)
    first_norm, first_pull = jax.vjp(layer_norm, inputs, norm1_gain, norm1_shift)
    grad_input_norm, grad_norm1_gain, grad_norm1_shift = first_pull(grad_normed)
    grad_tokens = grad_hidden + grad_input_norm
    column = lax.axis_index("tp")
    tp_count = lax.axis_size("tp")

    def widen(share_part):
        widened = jnp.zeros((share_part.shape[0] * tp_count,), jnp.float32)
        return lax.dynamic_update_slice_in_dim(widened, share_part, column * share_part.shape[0], 0)

    def narrow(widened, span_width):
        return lax.dynamic_slice_in_dim(widened, column * span_width, span_width, 0)

    summed = lax.psum(
        (
            grad_norm1_gain,
            grad_norm1_shift,
            widen(jnp.sum(grad_pre_query.astype(jnp.float32), axis=0)),
            widen(jnp.sum(grad_values.astype(jnp.float32), axis=0)),
            jnp.sum(grad_hidden, axis=0),
            grad_norm2_gain,
            grad_norm2_shift,
            widen(jnp.sum(grad_pre.astype(jnp.float32), axis=0)),
            jnp.sum(grad_output, axis=0),
        ),
        ("fsdp", "tp"),
    )
    return (
        output.astype(jnp.bfloat16),
        mean_loss,
        grad_tokens,
        summed[0],
        summed[1],
        grad_w_query,
        narrow(summed[2], b_query.shape[0]),
        grad_w_key,
        grad_w_value,
        narrow(summed[3], b_value.shape[0]),
        grad_w_out,
        summed[4],
        summed[5],
        summed[6],
        grad_w_up,
        narrow(summed[7], b_up.shape[0]),
        grad_w_down,
        summed[8],
    )


def solution(mesh):
    placed = (
        P(("fsdp", "tp"), None),
        P(),
        P(),
        P("fsdp", "tp"),
        P("tp"),
        P("fsdp", "tp"),
        P("fsdp", "tp"),
        P("tp"),
        P("fsdp", "tp"),
        P(),
        P(),
        P(),
        P("fsdp", "tp"),
        P("tp"),
        P("fsdp", "tp"),
        P(),
        P(("fsdp", "tp"), None),
        P(("fsdp", "tp")),
        P("fsdp", None),
        P("fsdp", None, None),
    )
    return jax.shard_map(
        body,
        mesh=mesh,
        in_specs=placed,
        out_specs=(
            P(("fsdp", "tp"), None),
            P(),
            P(("fsdp", "tp"), None),
            P(),
            P(),
            P("fsdp", "tp"),
            P("tp"),
            P("fsdp", "tp"),
            P("fsdp", "tp"),
            P("tp"),
            P("fsdp", "tp"),
            P(),
            P(),
            P(),
            P("fsdp", "tp"),
            P("tp"),
            P("fsdp", "tp"),
            P(),
        ),
        check_vma=False,
    )
```

profile of v0, /device:TPU:0, one launch (start us, length us, event | category | flops | bytes accessed | tf_op | source)
XLA Modules:
  0.0 1605.3 jit_solution(4273150163818574457)
XLA Ops:
  18.1 22.4 %all-gather.15.cloned.1.call-done = bf16[2048,512]{1,0:T(8,128)(2,1)} async-done(((bf16[256,512]{1,0:T(8,128)(2,1)}), bf16[2048,512]{1,0:T(8,128)(2,1)}) %all-gather.15.cloned.1.call-update) | async-done | bytes 2097168 | tf_op jit(solution)/shard_map/all_gather | solution.py:180
  40.6 82.9 %all-gather.11.cloned.1.call-done = bf16[1024,2048]{1,0:T(8,128)(2,1)} async-done(((bf16[256,2048]{1,0:T(8,128)(2,1)}), bf16[1024,2048]{1,0:T(8,128)(2,1)}) %all-gather.11.cloned.1.call-update) | async-done | bytes 4194320 | tf_op jit(solution)/shard_map/all_gather | solution.py:193
  123.5 5.2 convolution_convert_fusion.4
  128.7 22.9 %all-gather.17.cloned.1.call-done = bf16[2048,512]{1,0:T(8,128)(2,1)} async-done(((bf16[256,512]{1,0:T(8,128)(2,1)}), bf16[2048,512]{1,0:T(8,128)(2,1)}) %all-gather.17.cloned.1.call-update) | async-done | bytes 2097168 | tf_op jit(solution)/shard_map/all_gather | solution.py:181
  151.7 6.2 add_convert_fusion.1
  157.9 23.3 %all-gather.13.cloned.1.call-done = bf16[2048,512]{1,0:T(8,128)(2,1)} async-done(((bf16[256,512]{1,0:T(8,128)(2,1)}), bf16[2048,512]{1,0:T(8,128)(2,1)}) %all-gather.13.cloned.1.call-update) | async-done | bytes 2097168 | tf_op jit(solution)/shard_map/all_gather | solution.py:179
  181.2 5.2 multiply_convert_fusion.1
  187.5 34.3 %while.45 = (s32[]{:T(128)}, bf16[2,512,8,64]{1,3,2,0:T(8,128)(2,1)}, f32[2,8,512]{2,1,0:T(8,128)S(1)}, s32[2]{0:T(128)S(1)}, bf16[8,8]{1,0:T(8,128)(2,1)S(1)}, ...) while((s32[]{:T(128)}, ...), condition=%wide.region_9.10_spmd.clone, body=%wide.region_6.9_spmd.clone.sunk | while | flops 1123386368 | bytes 68315536 | solution.py:99
  192.1 2.9 select_reduce_fusion.2
  195.0 3.8 fusion.182
  198.8 5.0 fusion.183
  209.2 2.9 select_reduce_fusion.2
  212.1 3.8 fusion.182
  215.9 5.0 fusion.183
  221.9 2.7 copy.41
  224.9 7.6 fusion.97
  233.3 144.0 %reduce-scatter.11.cloned.1.call-done = f32[256,2048]{1,0:T(8,128)} async-done(((f32[1024,2048]{1,0:T(8,128)}), f32[256,2048]{1,0:T(8,128)}) %reduce-scatter.11.cloned.1.call-update) | async-done | bytes 2097168 | tf_op jit(solution)/shard_map/reduce_scatter | solution.py:206
  382.4 51.6 %all-gather.23.cloned.1.call-done = bf16[2048,2048]{1,0:T(8,128)(2,1)} async-done(((bf16[256,2048]{1,0:T(8,128)(2,1)}), bf16[2048,2048]{1,0:T(8,128)(2,1)}) %all-gather.23.cloned.1.call-update) | async-done | bytes 8388624 | tf_op jit(solution)/shard_map/all_gather | solution.py:187
  434.0 82.9 %all-gather.21.cloned.1.call-done = bf16[1024,2048]{1,0:T(8,128)(2,1)} async-done(((bf16[256,2048]{1,0:T(8,128)(2,1)}), bf16[1024,2048]{1,0:T(8,128)(2,1)}) %all-gather.21.cloned.1.call-update) | async-done | bytes 4194320 | tf_op jit(solution)/shard_map/all_gather | solution.py:211
  517.0 14.1 maximum_convert_fusion
  531.0 40.6 %all-gather.25.cloned.1.call-done = bf16[2048,2048]{1,0:T(8,128)(2,1)} async-done(((bf16[256,2048]{1,0:T(8,128)(2,1)}), bf16[2048,2048]{1,0:T(8,128)(2,1)}) %all-gather.25.cloned.1.call-update) | async-done | bytes 8388624 | tf_op jit(solution)/shard_map/all_gather | solution.py:188
  571.6 14.6 fusion.98
  587.5 44.5 %psum.78 = f32[]{:T(128)} all-reduce(f32[]{:T(128)} %convert_reduce_fusion.5), channel_id=1, replica_groups=mesh['fsdp'=8,'tp'=4] {'fsdp','tp'}, use_global_device_ids=true, to_apply=%region_17.18 | all-reduce | flops 1 | bytes 8 | tf_op jit(solution)/shard_map/psum | solution.py:222
  632.7 99.3 %reduce-scatter.13.cloned.1.call-done = f32[256,2048]{1,0:T(8,128)} async-done(((f32[1024,2048]{1,0:T(8,128)}), f32[256,2048]{1,0:T(8,128)}) %reduce-scatter.13.cloned.1.call-update) | async-done | bytes 2097168 | tf_op jit(solution)/shard_map/reduce_scatter | solution.py:216
  732.1 4.5 multiply_convert_fusion.2
  736.7 81.4 %all-gather.27.cloned.1.call-done = bf16[1024,2048]{1,0:T(8,128)(2,1)} async-done(((bf16[256,2048]{1,0:T(8,128)(2,1)}), bf16[1024,2048]{1,0:T(8,128)(2,1)}) %all-gather.27.cloned.1.call-update) | async-done | bytes 4194320 | tf_op jit(solution)/shard_map/all_gather | solution.py:229
  818.1 14.2 convert_reduce_fusion
  834.3 13.3 fusion.99
  847.7 143.2 %reduce-scatter.15.cloned.1.call-done = f32[256,2048]{1,0:T(8,128)} async-done(((f32[1024,2048]{1,0:T(8,128)}), f32[256,2048]{1,0:T(8,128)}) %reduce-scatter.15.cloned.1.call-update) | async-done | bytes 2097168 | tf_op jit(solution)/shard_map/reduce_scatter | solution.py:244
  990.9 3.0 multiply_reduce_fusion.1
  999.8 14.2 convolution_convert_fusion.2
  1014.1 14.1 convolution_convert_fusion.1
  1028.2 53.0 %all-gather.29.cloned.1.call-done = bf16[1024,2048]{1,0:T(8,128)(2,1)} async-done(((bf16[256,2048]{1,0:T(8,128)(2,1)}), bf16[1024,2048]{1,0:T(8,128)(2,1)}) %all-gather.29.cloned.1.call-update) | async-done | bytes 4194320 | tf_op jit(solution)/shard_map/all_gather | solution.py:250
  1081.2 6.2 convolution_convert_fusion.3
  1088.5 104.5 %while.47 = (s32[]{:T(128)}, f32[1024,8,64]{0,2,1:T(8,128)S(1)}, f32[1024,8,64]{0,2,1:T(8,128)}, bf16[2,512,8,64]{1,3,2,0:T(8,128)(2,1)}, s32[2]{0:T(128)S(1)}, ...) while((s32[]{:T(128)}, f32[1024,8,64]{0,2,1:T(8,128)S(1)}, ...), condition=%wide.region_23.24_spmd.clone, body=%wide.region_21.23_spmd.clone.sunk | while | flops 2748679168 | bytes 224012784 | solution.py:143
  1094.0 3.8 fusion.198
  1097.8 6.0 copy-done
  1103.8 5.7 bitcast_add_fusion.5
  1109.5 12.6 multiply_reduce_fusion.6
  1122.1 12.6 multiply_convert_fusion.4
  1134.7 2.7 fusion.200
  1144.6 3.6 fusion.198
  1148.2 5.8 copy-done
  1153.9 6.1 bitcast_add_fusion.5
  1160.0 15.1 multiply_reduce_fusion.6
  1175.2 12.8 multiply_convert_fusion.4
  1188.0 2.7 fusion.200
  1197.8 2.4 fusion.101
  1200.2 2.4 fusion.100
  1202.6 5.7 add_add_fusion
  1209.6 6.6 fusion.105
  1216.4 6.6 fusion.104
  1224.3 6.5 fusion.103
  1230.9 6.5 fusion.102
  1238.4 2.8 convert_element_type.150
  1241.3 2.9 convert_element_type.153
  1245.1 131.1 %reduce-scatter.17.cloned.1.call-done = f32[256,2048]{1,0:T(8,128)} async-done(((f32[1024,2048]{1,0:T(8,128)}), f32[256,2048]{1,0:T(8,128)}) %reduce-scatter.17.cloned.1.call-update) | async-done | bytes 2097168 | tf_op jit(solution)/shard_map/reduce_scatter | solution.py:274
  1376.3 2.3 fusion.92
  1379.6 43.3 %all-reduce.2 = (f32[]{:T(128)}, f32[2048]{0:T(1024)}, f32[2048]{0:T(1024)}, f32[2048]{0:T(1024)S(1)}, f32[2048]{0:T(1024)S(1)}, /*index=5*/f32[2048]{0:T(1024)}...) all-reduce(f32[]{:T(128)} %get-tuple-element.546, ...), channel_id=1, replica_groups=mesh['fsdp'=8,'tp'=4] {'fsdp','tp'}, use_global_device_ids=true, to_apply=%region_15.16 | all-reduce | flops 24577 | bytes 196616 | tf_op jit(solution)/shard_map/psum | solution.py:222
  1425.5 3.6 add_add_fusion.3
  1429.1 3.0 reduce-scatter.25.cloned.1.call-done
  1432.0 55.0 %reduce-scatter.23.cloned.1.call-done = f32[256,512]{1,0:T(8,128)} async-done(((f32[2048,512]{1,0:T(8,128)}), f32[256,512]{1,0:T(8,128)}) %reduce-scatter.23.cloned.1.call-update) | async-done | bytes 524304 | tf_op jit(solution)/shard_map/reduce_scatter | solution.py:266
  1487.0 55.1 %reduce-scatter.21.cloned.1.call-done = f32[256,512]{1,0:T(8,128)} async-done(((f32[2048,512]{1,0:T(8,128)}), f32[256,512]{1,0:T(8,128)}) %reduce-scatter.21.cloned.1.call-update) | async-done | bytes 524304 | tf_op jit(solution)/shard_map/reduce_scatter | solution.py:265
  1542.1 55.0 %reduce-scatter.19.cloned.1.call-done = f32[256,512]{1,0:T(8,128)} async-done(((f32[2048,512]{1,0:T(8,128)}), f32[256,512]{1,0:T(8,128)}) %reduce-scatter.19.cloned.1.call-update) | async-done | bytes 524304 | tf_op jit(solution)/shard_map/reduce_scatter | solution.py:264
  (260 shorter events, 59.4 us)
Async XLA Ops:
  7.2 5.1 copy-start.5
  7.2 5.1 copy-start.24
  7.2 5.1 copy-start.37
  7.2 33.3 %all-gather.15.cloned.1.call-start = ((), (), s32[]{:S(2)}) async-start(), calls=%async_computation.12 | async-start | bytes 2359296 | tf_op jit(solution)/shard_map/all_gather | solution.py:180
  8.0 115.5 %all-gather.11.cloned.1.call-start = ((), (), s32[]{:S(2)}) async-start(), calls=%async_computation.10 | async-start | bytes 5242880 | tf_op jit(solution)/shard_map/all_gather | solution.py:193
  9.5 2.2 copy-start.27
  11.7 4.0 copy-start.49
  11.7 6.3 copy-start.42
  13.7 137.9 %all-gather.17.cloned.1.call-start = ((), (), s32[]{:S(2)}) async-start(), calls=%async_computation.13 | async-start | bytes 2359296 | tf_op jit(solution)/shard_map/all_gather | solution.py:181
  14.5 166.8 %all-gather.13.cloned.1.call-start = ((), (), s32[]{:S(2)}) async-start(), calls=%async_computation.11 | async-start | bytes 2359296 | tf_op jit(solution)/shard_map/all_gather | solution.py:179
  15.0 209.8 %all-gather.19.cloned.1.call-start = ((), (), s32[]{:S(2)}) async-start(), calls=%async_computation.14 | async-start | bytes 2359296 | tf_op jit(solution)/shard_map/all_gather | solution.py:182
  15.6 361.6 %reduce-scatter.11.cloned.1.call-start = ((), (), s32[]{:S(2)}) async-start(), calls=%async_computation.15 | async-start | bytes 10485760 | tf_op jit(solution)/shard_map/reduce_scatter | solution.py:206
  18.1 133.5 %copy-start.47 = (f32[512]{0:T(512)S(1)}, f32[512]{0:T(512)}, u32[]{:S(2)}) copy-start(f32[512]{0:T(512)} %param.33) | copy-start | bytes 6148
  128.7 52.5 %copy-start.48 = (f32[512]{0:T(512)S(1)}, f32[512]{0:T(512)}, u32[]{:S(2)}) copy-start(f32[512]{0:T(512)} %param.30) | copy-start | bytes 6148
  195.0 3.8 copy-start.7
  195.0 3.8 copy-start.17
  212.1 3.8 copy-start.7
  212.1 3.8 copy-start.17
  221.9 10.6 copy-start.3
  224.8 7.6 copy-start.22
  232.4 144.8 %copy-start.38 = (f32[2048]{0:T(1024)S(1)}, f32[2048]{0:T(1024)}, u32[]{:S(2)}) copy-start(f32[2048]{0:T(1024)} %param.35) | copy-start | bytes 24580
  232.5 201.6 %all-gather.23.cloned.1.call-start = ((), (), s32[]{:S(2)}) async-start(), calls=%async_computation.17 | async-start | bytes 9437184 | tf_op jit(solution)/shard_map/all_gather | solution.py:187
  233.2 283.7 %all-gather.21.cloned.1.call-start = ((), (), s32[]{:S(2)}) async-start(), calls=%async_computation.16 | async-start | bytes 5242880 | tf_op jit(solution)/shard_map/all_gather | solution.py:211
  380.2 136.8 %copy-start.46 = (f32[2048]{0:T(1024)S(1)}, f32[2048]{0:T(1024)}, u32[]{:S(2)}) copy-start(f32[2048]{0:T(1024)} %param.39) | copy-start | bytes 24580
  381.6 190.0 %all-gather.25.cloned.1.call-start = ((), (), s32[]{:S(2)}) async-start(), calls=%async_computation.18 | async-start | bytes 9437184 | tf_op jit(solution)/shard_map/all_gather | solution.py:188
  382.4 349.7 %reduce-scatter.13.cloned.1.call-start = ((), (), s32[]{:S(2)}) async-start(), calls=%async_computation.19 | async-start | bytes 10485760 | tf_op jit(solution)/shard_map/reduce_scatter | solution.py:216
  586.2 145.8 %copy-start.41 = (f32[2048]{0:T(1024)S(1)}, f32[2048]{0:T(1024)}, u32[]{:S(2)}) copy-start(f32[2048]{0:T(1024)} %param.41) | copy-start | bytes 24580
  586.3 231.8 %all-gather.27.cloned.1.call-start = ((), (), s32[]{:S(2)}) async-start(), calls=%async_computation.20 | async-start | bytes 5242880 | tf_op jit(solution)/shard_map/all_gather | solution.py:229
  736.6 254.3 %reduce-scatter.15.cloned.1.call-start = ((), (), s32[]{:S(2)}) async-start(), calls=%async_computation.21 | async-start | bytes 10485760 | tf_op jit(solution)/shard_map/reduce_scatter | solution.py:244
  832.3 2.0 copy-start.50
  847.6 233.6 %all-gather.29.cloned.1.call-start = ((), (), s32[]{:S(2)}) async-start(), calls=%async_computation.22 | async-start | bytes 5242880 | tf_op jit(solution)/shard_map/all_gather | solution.py:250
  990.9 3.1 copy-start.15
  994.0 1.6 copy-start.16
  999.7 238.7 %reduce-scatter.27.cloned.1.call-start = ((), (), s32[]{:S(2)}) async-start(), calls=%async_computation.28 | async-start | bytes 9437184 | tf_op jit(solution)/shard_map/reduce_scatter | solution.py:237
  1014.0 227.3 %reduce-scatter.29.cloned.1.call-start = ((), (), s32[]{:S(2)}) async-start(), calls=%async_computation.29 | async-start | bytes 9437184 | tf_op jit(solution)/shard_map/reduce_scatter | solution.py:240
  1028.2 348.1 %reduce-scatter.17.cloned.1.call-start = ((), (), s32[]{:S(2)}) async-start(), calls=%async_computation.23 | async-start | bytes 10485760 | tf_op jit(solution)/shard_map/reduce_scatter | solution.py:274
  1094.0 9.8 copy-start.1
  1097.8 6.0 copy-start
  1122.0 12.6 copy-start.11
  1134.7 2.7 copy-start.4
  1137.4 1.9 copy-start.12
  1144.6 9.4 copy-start.1
  1148.1 5.8 copy-start
  1175.2 12.8 copy-start.11
  1188.0 2.7 copy-start.4
  1190.6 2.0 copy-start.12
  1193.1 1.5 copy-start.13
  1193.3 3.5 copy-start.20
  1194.7 1.8 copy-start.2
  1196.1 1.7 copy-start.44
  1197.8 2.4 copy-start.45
  1200.2 2.4 copy-start.19
  1208.4 223.7 %reduce-scatter.25.cloned.1.call-start = ((), (), s32[]{:S(2)}) async-start(), calls=%async_computation.27 | async-start | bytes 4718592 | tf_op jit(solution)/shard_map/reduce_scatter | solution.py:267
  1216.2 270.8 %reduce-scatter.23.cloned.1.call-start = ((), (), s32[]{:S(2)}) async-start(), calls=%async_computation.26 | async-start | bytes 4718592 | tf_op jit(solution)/shard_map/reduce_scatter | solution.py:266
  1223.0 319.1 %reduce-scatter.21.cloned.1.call-start = ((), (), s32[]{:S(2)}) async-start(), calls=%async_computation.25 | async-start | bytes 4718592 | tf_op jit(solution)/shard_map/reduce_scatter | solution.py:265
  1230.8 366.3 %reduce-scatter.19.cloned.1.call-start = ((), (), s32[]{:S(2)}) async-start(), calls=%async_computation.24 | async-start | bytes 4718592 | tf_op jit(solution)/shard_map/reduce_scatter | solution.py:264
  1241.2 3.0 copy-start.14
  1241.3 135.0 %copy-start.6 = (bf16[256,2048]{1,0:T(8,128)(2,1)S(1)}, bf16[256,2048]{1,0:T(8,128)(2,1)}, u32[]{:S(2)}) copy-start(bf16[256,2048]{1,0:T(8,128)(2,1)} %param.26) | copy-start | bytes 3145732
  1241.3 135.0 %copy-start.25 = (f32[2048]{0:T(1024)S(1)}, f32[2048]{0:T(1024)}, u32[]{:S(2)}) copy-start(f32[2048]{0:T(1024)} %param.27) | copy-start | bytes 24580
  1241.3 135.0 %copy-start.28 = (f32[256]{0:T(256)S(1)}, f32[256]{0:T(256)}, u32[]{:S(2)}) copy-start(f32[256]{0:T(256)} %copy-done.27) | copy-start | bytes 3076
  1244.2 134.4 %copy-start.36 = (f32[256]{0:T(256)S(1)}, f32[256]{0:T(256)}, u32[]{:S(2)}) copy-start(f32[256]{0:T(256)} %copy-done.35) | copy-start | bytes 3076
  1244.2 134.4 %copy-start.34 = (f32[256]{0:T(256)S(1)}, f32[256]{0:T(256)}, u32[]{:S(2)}) copy-start(f32[256]{0:T(256)} %copy-done.33) | copy-start | bytes 3076
  1376.3 2.4 copy-start.10
  1378.6 46.9 %copy-start.9 = (f32[256,2048]{1,0:T(8,128)S(1)}, f32[256,2048]{1,0:T(8,128)}, u32[]{:S(2)}) copy-start(f32[256,2048]{1,0:T(8,128)} %copy-done.8) | copy-start | bytes 6291460
  (15 other events, 13.9 us)
Sparse Core Ops, SparseCore 0:
  9.9 30.5 all-gather.14
  42.7 80.7 all-gather.10
  125.4 26.2 all-gather.16
  153.4 27.7 all-gather.12
  183.0 27.7 all-gather.18
  232.6 144.6 reduce-scatter.10
  379.1 54.8 all-gather.22
  436.2 80.7 all-gather.20
  518.9 52.7 all-gather.24
  586.4 145.6 reduce-scatter.12
  736.7 81.2 all-gather.26
  847.8 143.0 reduce-scatter.14
  999.8 81.3 all-gather.28
  1084.6 69.9 reduce-scatter.26
  1157.9 71.4 reduce-scatter.28
  1231.6 144.6 reduce-scatter.16
  1380.0 51.9 reduce-scatter.24
  1435.8 51.1 reduce-scatter.22
  1490.9 51.1 reduce-scatter.20
  1545.9 51.1 reduce-scatter.18
where the time goes:
time: 1610 us
  waiting for transfers between devices  1150 us (71%)
  matrix products  230 us (14%)
  blocking collectives  87.8 us (5%)
  other arithmetic  71.4 us (4%)
  local copies, waits for them, and re-layouts  37 us (2%)
  between operations  18.2 us (1%)
    reduce_scatter x1, waiting for transfers between devices, body(): lax.psum_scatter(contract(attended, full_out, 1, 1), 'tp', scatter_dimens...  144 us
    reduce_scatter x1, waiting for transfers between devices, body(): lax.psum_scatter(contract(grad_pre, full_up, 1, 1), 'tp', scatter_dimensi...  143 us
    reduce_scatter x1, waiting for transfers between devices, body(): lax.psum_scatter(grad_normed, 'tp', scatter_dimension=0, tiled=True)  131 us
    dot_general x12, matrix products, contract(): lax.dot_general(left_side, right_side, (((left_dim,), (right_dim,)), ((),...  101 us
    reduce_scatter x1, waiting for transfers between devices, body(): lax.psum_scatter(contract(active, full_down, 1, 1), 'tp', scatter_dimensi...  99.3 us
    psum x2, blocking collectives, body(): lax.psum((jnp.sum(weight_mask), jnp.sum(weight_mask[:, None] * deviation...  87.8 us
    all_gather x1, waiting for transfers between devices, body(): normed_all = lax.all_gather(normed, 'tp', axis=0, tiled=True)  82.9 us
    all_gather x1, waiting for transfers between devices, body(): normed_mid_all = lax.all_gather(normed_mid, 'tp', axis=0, tiled=True)  82.9 us
  transfers between devices with their start and end apart: 20, of which 17 were waited for; matrix products, arithmetic and copies ran while one was open for 16% of the time, Pallas kernels for 0%

commit v1 on v0

--- a/solution.py
+++ b/solution.py
@@ -6,6 +6,28 @@
 HD = 64
 EPSILON = 1e-05
 MASKED_SCORE = -1e30
+
+
+def joined_along(blocks, dim):
+    blocks = jnp.moveaxis(blocks, 0, dim)
+    shape = blocks.shape
+    return blocks.reshape(*shape[:dim], shape[dim] * shape[dim + 1], *shape[dim + 2 :])
+
+
+def ring_gather(array, axis, dim):
+    size = lax.axis_size(axis)
+    pairs = [(i, (i + 1) % size) for i in range(size)]
+    back = [(b, a) for a, b in pairs]
+    lower, upper = ([], [])
+    for hop in range(size - 1):
+        if hop % 2 == 0:
+            lower.append(lax.ppermute(lower[-1] if lower else array, axis, pairs))
+        else:
+            upper.append(lax.ppermute(upper[-1] if upper else array, axis, back))
+    blocks = jnp.stack([*lower[::-1], array, *upper])
+    shift = lax.axis_index(axis) - len(lower)
+    blocks = blocks[(jnp.arange(size) - shift) % size]
+    return joined_along(blocks, dim)
 
 
 def layer_norm(vectors, norm_gain, norm_shift):
@@ -183,10 +205,7 @@
         )
 
     def feed_weights():
-        return (
-            lax.all_gather(w_up, "fsdp", axis=0, tiled=True),
-            lax.all_gather(w_down, "fsdp", axis=0, tiled=True),
-        )
+        return (ring_gather(w_up, "fsdp", 0), lax.all_gather(w_down, "fsdp", axis=0, tiled=True))
 
     inputs = tokens.astype(jnp.float32)
     normed = layer_norm(inputs, norm1_gain, norm1_shift).astype(jnp.bfloat16)

time: 1610 us -> 1560 us (0.969)
  waiting for transfers between devices: 1150 us -> 1060 us
  local copies, waits for them, and re-layouts: 37 us -> 57.3 us
    ppermute x0 -> x7, waiting for transfers between devices: none -> 85.1 us  [the longest x4 85.1 us: ring_gather(): lower.append(lax.ppermute(lower[-1] if lower else array, axis, pairs))]
    all_gather x1, waiting for transfers between devices: 82.9 us -> 0.01 us  [body(): normed_mid_all = lax.all_gather(normed_mid, 'tp', axis=0, tiled=True)]
    all_gather x1 -> x0, waiting for transfers between devices: 51.6 us -> none  [feed_weights(): lax.all_gather(w_up, 'fsdp', axis=0, tiled=True)]
    all_gather x1, waiting for transfers between devices: 40.6 us -> 5.61 us  [feed_weights(): lax.all_gather(w_down, 'fsdp', axis=0, tiled=True)]
  transfers between devices with their start and end apart: 20 -> 26, of which waited for: 17 -> 19; matrix products, arithmetic and copies ran while one was open for 16% -> 18% of each run, Pallas kernels for 0% -> 0%
where the time goes in v1:
time: 1560 us; the launch traced here: 1550 us
  waiting for transfers between devices  1060 us (68%)
  matrix products  230 us (15%)
  blocking collectives  87.7 us (6%)
  other arithmetic  75.2 us (5%)
  local copies, waits for them, and re-layouts  57.3 us (4%)
  between operations  18.2 us (1%)
    reduce_scatter x1, waiting for transfers between devices, body(): lax.psum_scatter(contract(attended, full_out, 1, 1), 'tp', scatter_dimens...  145 us
    reduce_scatter x1, waiting for transfers between devices, body(): lax.psum_scatter(contract(grad_pre, full_up, 1, 1), 'tp', scatter_dimensi...  143 us
    reduce_scatter x1, waiting for transfers between devices, body(): lax.psum_scatter(grad_normed, 'tp', scatter_dimension=0, tiled=True)  130 us
    dot_general x12, matrix products, contract(): lax.dot_general(left_side, right_side, (((left_dim,), (right_dim,)), ((),...  101 us
    reduce_scatter x1, waiting for transfers between devices, body(): lax.psum_scatter(contract(active, full_down, 1, 1), 'tp', scatter_dimensi...  99.3 us
    psum x2, blocking collectives, body(): lax.psum((jnp.sum(weight_mask), jnp.sum(weight_mask[:, None] * deviation...  87.7 us
    ppermute x4, waiting for transfers between devices, ring_gather(): lower.append(lax.ppermute(lower[-1] if lower else array, axis, pairs))  85.1 us
    all_gather x1, waiting for transfers between devices, body(): normed_all = lax.all_gather(normed, 'tp', axis=0, tiled=True)  82.9 us
  transfers between devices with their start and end apart: 26, of which 19 were waited for; matrix products, arithmetic and copies ran while one was open for 18% of the time, Pallas kernels for 0%

profile of v1, /device:TPU:0, one launch (start us, length us, event | category | flops | bytes accessed | tf_op | source)
XLA Modules:
  0.0 1551.0 jit_solution(291893287170971777)
XLA Ops:
  12.3 2.7 fusion.79
  19.4 21.2 %all-gather.14.cloned.1.call-done = bf16[2048,512]{1,0:T(8,128)(2,1)} async-done(((bf16[256,512]{1,0:T(8,128)(2,1)}), bf16[2048,512]{1,0:T(8,128)(2,1)}) %all-gather.14.cloned.1.call-update) | async-done | bytes 2097168 | tf_op jit(solution)/shard_map/all_gather | solution.py:202
  40.5 82.9 %all-gather.10.cloned.1.call-done = bf16[1024,2048]{1,0:T(8,128)(2,1)} async-done(((bf16[256,2048]{1,0:T(8,128)(2,1)}), bf16[1024,2048]{1,0:T(8,128)(2,1)}) %all-gather.10.cloned.1.call-update) | async-done | bytes 4194320 | tf_op jit(solution)/shard_map/all_gather | solution.py:212
  123.4 5.2 convolution_convert_fusion.4
  128.7 22.9 %all-gather.16.cloned.1.call-done = bf16[2048,512]{1,0:T(8,128)(2,1)} async-done(((bf16[256,512]{1,0:T(8,128)(2,1)}), bf16[2048,512]{1,0:T(8,128)(2,1)}) %all-gather.16.cloned.1.call-update) | async-done | bytes 2097168 | tf_op jit(solution)/shard_map/all_gather | solution.py:203
  151.6 6.2 add_convert_fusion.1
  157.9 23.3 %all-gather.12.cloned.1.call-done = bf16[2048,512]{1,0:T(8,128)(2,1)} async-done(((bf16[256,512]{1,0:T(8,128)(2,1)}), bf16[2048,512]{1,0:T(8,128)(2,1)}) %all-gather.12.cloned.1.call-update) | async-done | bytes 2097168 | tf_op jit(solution)/shard_map/all_gather | solution.py:201
  181.2 5.2 multiply_convert_fusion.1
  187.5 34.4 %while.45 = (s32[]{:T(128)}, bf16[2,512,8,64]{1,3,2,0:T(8,128)(2,1)}, f32[2,8,512]{2,1,0:T(8,128)S(1)}, s32[2]{0:T(128)S(1)}, bf16[8,8]{1,0:T(8,128)(2,1)S(1)}, ...) while((s32[]{:T(128)}, ...), condition=%wide.region_9.10_spmd.clone, body=%wide.region_6.9_spmd.clone.sunk | while | flops 1123386368 | bytes 68315536 | solution.py:121
  192.1 2.9 select_reduce_fusion.2
  195.0 3.8 fusion.184
  198.8 5.0 fusion.185
  209.2 2.9 select_reduce_fusion.2
  212.1 3.8 fusion.184
  215.9 5.0 fusion.185
  221.9 3.1 copy.41
  225.3 7.6 fusion.99
  233.1 144.7 %reduce-scatter.11.cloned.1.call-done = f32[256,2048]{1,0:T(8,128)} async-done(((f32[1024,2048]{1,0:T(8,128)}), f32[256,2048]{1,0:T(8,128)}) %reduce-scatter.11.cloned.1.call-update) | async-done | bytes 2097168 | tf_op jit(solution)/shard_map/reduce_scatter | solution.py:225
  382.4 15.1 collective-permute-done
  400.2 22.8 %collective-permute-done.1 = bf16[256,2048]{1,0:T(8,128)(2,1)S(1)} collective-permute-done((bf16[256,2048]{1,0:T(8,128)(2,1)S(1)}, bf16[256,2048]{1,0:T(8,128)(2,1)S(1)}, u32[]{:S(2)}, u32[]{:S(2)}) %collective-permute-start.1) | collective-permute-done | bytes 1048608 | tf_op jit(solution)/shard_map/ppermute | solution.py:24
  425.7 23.2 %collective-permute-done.2 = bf16[256,2048]{1,0:T(8,128)(2,1)} collective-permute-done((bf16[256,2048]{1,0:T(8,128)(2,1)S(1)}, bf16[256,2048]{1,0:T(8,128)(2,1)}, u32[]{:S(2)}, u32[]{:S(2)}) %collective-permute-start.2) | collective-permute-done | bytes 1048608 | tf_op jit(solution)/shard_map/ppermute | solution.py:24
  449.0 2.9 collective-permute-start.6
  451.9 24.0 %collective-permute-done.3 = bf16[256,2048]{1,0:T(8,128)(2,1)} collective-permute-done((bf16[256,2048]{1,0:T(8,128)(2,1)}, bf16[256,2048]{1,0:T(8,128)(2,1)}, u32[]{:S(2)}, u32[]{:S(2)}) %collective-permute-start.3) | collective-permute-done | bytes 1048608 | tf_op jit(solution)/shard_map/ppermute | solution.py:24
  489.4 9.1 gather_fusion
  498.5 14.0 maximum_convert_fusion
  512.5 5.6 all-gather.22.cloned.1.call-done
  518.1 14.7 fusion.100
  534.1 44.5 %psum.78 = f32[]{:T(128)} all-reduce(f32[]{:T(128)} %convert_reduce_fusion.5), channel_id=1, replica_groups=mesh['fsdp'=8,'tp'=4] {'fsdp','tp'}, use_global_device_ids=true, to_apply=%region_17.18 | all-reduce | flops 1 | bytes 8 | tf_op jit(solution)/shard_map/psum | solution.py:241
  579.3 99.3 %reduce-scatter.13.cloned.1.call-done = f32[256,2048]{1,0:T(8,128)} async-done(((f32[1024,2048]{1,0:T(8,128)}), f32[256,2048]{1,0:T(8,128)}) %reduce-scatter.13.cloned.1.call-update) | async-done | bytes 2097168 | tf_op jit(solution)/shard_map/reduce_scatter | solution.py:235
  678.6 4.2 multiply_convert_fusion.2
  683.3 81.0 %all-gather.24.cloned.1.call-done = bf16[1024,2048]{1,0:T(8,128)(2,1)} async-done(((bf16[256,2048]{1,0:T(8,128)(2,1)}), bf16[1024,2048]{1,0:T(8,128)(2,1)}) %all-gather.24.cloned.1.call-update) | async-done | bytes 4194320 | tf_op jit(solution)/shard_map/all_gather | solution.py:248
  764.3 13.8 convert_reduce_fusion
  780.2 13.4 fusion.101
  793.6 143.2 %reduce-scatter.15.cloned.1.call-done = f32[256,2048]{1,0:T(8,128)} async-done(((f32[1024,2048]{1,0:T(8,128)}), f32[256,2048]{1,0:T(8,128)}) %reduce-scatter.15.cloned.1.call-update) | async-done | bytes 2097168 | tf_op jit(solution)/shard_map/reduce_scatter | solution.py:263
  936.8 3.0 multiply_reduce_fusion.1
  945.8 14.1 convolution_convert_fusion.2
  960.0 14.1 convolution_convert_fusion.1
  974.2 52.9 %all-gather.26.cloned.1.call-done = bf16[1024,2048]{1,0:T(8,128)(2,1)} async-done(((bf16[256,2048]{1,0:T(8,128)(2,1)}), bf16[1024,2048]{1,0:T(8,128)(2,1)}) %all-gather.26.cloned.1.call-update) | async-done | bytes 4194320 | tf_op jit(solution)/shard_map/all_gather | solution.py:269
  1027.1 6.2 convolution_convert_fusion.3
  1034.4 104.6 %while.47 = (s32[]{:T(128)}, f32[1024,8,64]{0,2,1:T(8,128)S(1)}, f32[1024,8,64]{0,2,1:T(8,128)}, bf16[2,512,8,64]{1,3,2,0:T(8,128)(2,1)}, s32[2]{0:T(128)S(1)}, ...) while((s32[]{:T(128)}, f32[1024,8,64]{0,2,1:T(8,128)S(1)}, ...), condition=%wide.region_23.24_spmd.clone, body=%wide.region_21.23_spmd.clone.sunk | while | flops 2748679168 | bytes 224012784 | solution.py:165
  1039.9 3.8 fusion.200
  1043.7 6.0 copy-done
  1049.7 5.7 bitcast_add_fusion.5
  1055.4 12.6 multiply_reduce_fusion.6
  1068.0 12.6 multiply_convert_fusion.4
  1090.5 3.6 fusion.200
  1094.1 5.8 copy-done
  1099.9 6.1 bitcast_add_fusion.5
  1106.0 15.2 multiply_reduce_fusion.6
  1121.1 12.8 multiply_convert_fusion.4
  1147.8 5.8 add_add_fusion
  1154.8 6.7 fusion.107
  1161.7 6.6 fusion.106
  1169.6 6.6 fusion.105
  1176.3 6.5 fusion.104
  1184.0 2.9 convert_element_type.150
  1186.9 2.8 convert_element_type.153
  1192.0 130.4 %reduce-scatter.17.cloned.1.call-done = f32[256,2048]{1,0:T(8,128)} async-done(((f32[1024,2048]{1,0:T(8,128)}), f32[256,2048]{1,0:T(8,128)}) %reduce-scatter.17.cloned.1.call-update) | async-done | bytes 2097168 | tf_op jit(solution)/shard_map/reduce_scatter | solution.py:293
  1325.7 43.1 %all-reduce.2 = (f32[]{:T(128)}, f32[2048]{0:T(1024)}, f32[2048]{0:T(1024)}, f32[2048]{0:T(1024)S(1)}, f32[2048]{0:T(1024)S(1)}, /*index=5*/f32[2048]{0:T(1024)}...) all-reduce(f32[]{:T(128)} %get-tuple-element.546, ...), channel_id=1, replica_groups=mesh['fsdp'=8,'tp'=4] {'fsdp','tp'}, use_global_device_ids=true, to_apply=%region_15.16 | all-reduce | flops 24577 | bytes 196616 | tf_op jit(solution)/shard_map/psum | solution.py:241
  1371.4 3.6 add_add_fusion.3
  1375.1 3.0 reduce-scatter.25.cloned.1.call-done
  1378.1 55.0 %reduce-scatter.23.cloned.1.call-done = f32[256,512]{1,0:T(8,128)} async-done(((f32[2048,512]{1,0:T(8,128)}), f32[256,512]{1,0:T(8,128)}) %reduce-scatter.23.cloned.1.call-update) | async-done | bytes 524304 | tf_op jit(solution)/shard_map/reduce_scatter | solution.py:285
  1433.1 55.0 %reduce-scatter.21.cloned.1.call-done = f32[256,512]{1,0:T(8,128)} async-done(((f32[2048,512]{1,0:T(8,128)}), f32[256,512]{1,0:T(8,128)}) %reduce-scatter.21.cloned.1.call-update) | async-done | bytes 524304 | tf_op jit(solution)/shard_map/reduce_scatter | solution.py:284
  1488.0 55.1 %reduce-scatter.19.cloned.1.call-done = f32[256,512]{1,0:T(8,128)} async-done(((f32[2048,512]{1,0:T(8,128)}), f32[256,512]{1,0:T(8,128)}) %reduce-scatter.19.cloned.1.call-update) | async-done | bytes 524304 | tf_op jit(solution)/shard_map/reduce_scatter | solution.py:283
  (310 shorter events, 89.1 us)
Async XLA Ops:
  7.2 9.8 copy-start.61
  7.2 12.0 copy-start.52
  7.2 33.3 %all-gather.14.cloned.1.call-start = ((), (), s32[]{:S(2)}) async-start(), calls=%async_computation.12 | async-start | bytes 2359296 | tf_op jit(solution)/shard_map/all_gather | solution.py:202
  7.9 115.5 %all-gather.10.cloned.1.call-start = ((), (), s32[]{:S(2)}) async-start(), calls=%async_computation.10 | async-start | bytes 5242880 | tf_op jit(solution)/shard_map/all_gather | solution.py:212
  14.9 136.7 %all-gather.16.cloned.1.call-start = ((), (), s32[]{:S(2)}) async-start(), calls=%async_computation.13 | async-start | bytes 2359296 | tf_op jit(solution)/shard_map/all_gather | solution.py:203
  15.7 165.5 %all-gather.12.cloned.1.call-start = ((), (), s32[]{:S(2)}) async-start(), calls=%async_computation.11 | async-start | bytes 2359296 | tf_op jit(solution)/shard_map/all_gather | solution.py:201
  16.3 209.0 %all-gather.18.cloned.1.call-start = ((), (), s32[]{:S(2)}) async-start(), calls=%async_computation.14 | async-start | bytes 2359296 | tf_op jit(solution)/shard_map/all_gather | solution.py:204
  16.9 360.9 %reduce-scatter.11.cloned.1.call-start = ((), (), s32[]{:S(2)}) async-start(), calls=%async_computation.15 | async-start | bytes 10485760 | tf_op jit(solution)/shard_map/reduce_scatter | solution.py:225
  19.3 132.3 %copy-start.59 = (f32[512]{0:T(512)S(1)}, f32[512]{0:T(512)}, u32[]{:S(2)}) copy-start(f32[512]{0:T(512)} %param.33) | copy-start | bytes 6148
  128.7 52.5 %copy-start.60 = (f32[512]{0:T(512)S(1)}, f32[512]{0:T(512)}, u32[]{:S(2)}) copy-start(f32[512]{0:T(512)} %param.30) | copy-start | bytes 6148
  221.9 11.0 copy-start.1
  221.9 11.2 copy-start.5
  225.3 7.7 copy-start.23
  232.9 144.8 %copy-start.7 = (bf16[256,2048]{1,0:T(8,128)(2,1)S(1)}, bf16[256,2048]{1,0:T(8,128)(2,1)}, u32[]{:S(2)}) copy-start(bf16[256,2048]{1,0:T(8,128)(2,1)} %param.26) | copy-start | bytes 3145732
  232.9 144.8 %copy-start.48 = (f32[2048]{0:T(1024)S(1)}, f32[2048]{0:T(1024)}, u32[]{:S(2)}) copy-start(f32[2048]{0:T(1024)} %param.35) | copy-start | bytes 24580
  233.0 147.1 %copy-start.35 = (f32[2048]{0:T(1024)S(1)}, f32[2048]{0:T(1024)}, u32[]{:S(2)}) copy-start(f32[2048]{0:T(1024)} %param.36) | copy-start | bytes 24580
  233.0 147.1 %copy-start.49 = (f32[2048]{0:T(1024)S(1)}, f32[2048]{0:T(1024)}, u32[]{:S(2)}) copy-start(f32[2048]{0:T(1024)} %param.37) | copy-start | bytes 24580
  233.0 265.5 %all-gather.20.cloned.1.call-start = ((), (), s32[]{:S(2)}) async-start(), calls=%async_computation.16 | async-start | bytes 5242880 | tf_op jit(solution)/shard_map/all_gather | solution.py:230
  381.6 136.5 %all-gather.22.cloned.1.call-start = ((), (), s32[]{:S(2)}) async-start(), calls=%async_computation.17 | async-start | bytes 9437184 | tf_op jit(solution)/shard_map/all_gather | solution.py:208
  382.3 296.3 %reduce-scatter.13.cloned.1.call-start = ((), (), s32[]{:S(2)}) async-start(), calls=%async_computation.18 | async-start | bytes 10485760 | tf_op jit(solution)/shard_map/reduce_scatter | solution.py:235
  382.4 15.2 collective-permute-start
  397.5 25.5 %copy-start.25 = (bf16[256,2048]{1,0:T(8,128)(2,1)}, bf16[256,2048]{1,0:T(8,128)(2,1)S(1)}, u32[]{:S(2)}) copy-start(bf16[256,2048]{1,0:T(8,128)(2,1)S(1)} %collective-permute-done) | copy-start | bytes 3145732
  397.5 25.5 %collective-permute-start.1 = (bf16[256,2048]{1,0:T(8,128)(2,1)S(1)}, bf16[256,2048]{1,0:T(8,128)(2,1)S(1)}, u32[]{:S(2)}, u32[]{:S(2)}) collective-permute-start(bf16[256,2048]{1,0:T(8,128)(2,1)S(1)} %collective-permute-done), channel_id=1, source_target_pairs={{0,4},{4,8},{8,12},{12,16},{16,20},{20,24},{24,28},{28,0},{1,5},{5... | collective-permute-start | bytes 3145736 | tf_op jit(solution)/shard_map/ppermute | solution.py:24
  397.6 25.5 %collective-permute-start.4 = (bf16[256,2048]{1,0:T(8,128)(2,1)S(1)}, bf16[256,2048]{1,0:T(8,128)(2,1)}, u32[]{:S(2)}, u32[]{:S(2)}) collective-permute-start(bf16[256,2048]{1,0:T(8,128)(2,1)S(1)} %copy-done.22), channel_id=1, source_target_pairs={{4,0},{8,4},{12,8},{16,12},{20,16},{24,20},{28,24},{0,28},{5,1},{9... | collective-permute-start | bytes 3145736 | tf_op jit(solution)/shard_map/ppermute | solution.py:26
  423.0 25.9 %collective-permute-start.2 = (bf16[256,2048]{1,0:T(8,128)(2,1)S(1)}, bf16[256,2048]{1,0:T(8,128)(2,1)}, u32[]{:S(2)}, u32[]{:S(2)}) collective-permute-start(bf16[256,2048]{1,0:T(8,128)(2,1)S(1)} %collective-permute-done.1), channel_id=1, source_target_pairs={{0,4},{4,8},{8,12},{12,16},{16,20},{20,24},{24,28},{28,0},{1,5},{5... | collective-permute-start | bytes 3145736 | tf_op jit(solution)/shard_map/ppermute | solution.py:24
  423.1 25.9 %collective-permute-start.5 = (bf16[256,2048]{1,0:T(8,128)(2,1)}, bf16[256,2048]{1,0:T(8,128)(2,1)}, u32[]{:S(2)}, u32[]{:S(2)}) collective-permute-start(bf16[256,2048]{1,0:T(8,128)(2,1)} %collective-permute-done.4), channel_id=1, source_target_pairs={{4,0},{8,4},{12,8},{16,12},{20,16},{24,20},{28,24},{0,28},{5,1},{9... | collective-permute-start | bytes 3145736 | tf_op jit(solution)/shard_map/ppermute | solution.py:26
  448.9 26.9 %collective-permute-start.3 = (bf16[256,2048]{1,0:T(8,128)(2,1)}, bf16[256,2048]{1,0:T(8,128)(2,1)}, u32[]{:S(2)}, u32[]{:S(2)}) collective-permute-start(bf16[256,2048]{1,0:T(8,128)(2,1)} %collective-permute-done.2), channel_id=1, source_target_pairs={{0,4},{4,8},{8,12},{12,16},{16,20},{20,24},{24,28},{28,0},{1,5},{5... | collective-permute-start | bytes 3145736 | tf_op jit(solution)/shard_map/ppermute | solution.py:24
  448.9 31.5 %copy-start.28 = (bf16[256,2048]{1,0:T(8,128)(2,1)S(1)}, bf16[256,2048]{1,0:T(8,128)(2,1)}, u32[]{:S(2)}) copy-start(bf16[256,2048]{1,0:T(8,128)(2,1)} %copy-done.27) | copy-start | bytes 3145732
  448.9 32.6 %copy-start.26 = (bf16[256,2048]{1,0:T(8,128)(2,1)S(1)}, bf16[256,2048]{1,0:T(8,128)(2,1)}, u32[]{:S(2)}) copy-start(bf16[256,2048]{1,0:T(8,128)(2,1)} %copy-done.25) | copy-start | bytes 3145732
  449.0 39.3 %collective-permute-start.6 = (bf16[256,2048]{1,0:T(8,128)(2,1)}, bf16[256,2048]{1,0:T(8,128)(2,1)S(1)}, u32[]{:S(2)}, u32[]{:S(2)}) collective-permute-start(bf16[256,2048]{1,0:T(8,128)(2,1)} %collective-permute-done.5), channel_id=1, source_target_pairs={{4,0},{8,4},{12,8},{16,12},{20,16},{24,20},{28,24},{0,28},{5,1},{9... | collective-permute-start | bytes 3145736 | tf_op jit(solution)/shard_map/ppermute | solution.py:26
  489.4 9.1 copy-start.58
  532.8 145.8 %copy-start.29 = (bf16[256,2048]{1,0:T(8,128)(2,1)S(1)}, bf16[256,2048]{1,0:T(8,128)(2,1)}, u32[]{:S(2)}) copy-start(bf16[256,2048]{1,0:T(8,128)(2,1)} %param.42) | copy-start | bytes 3145732
  532.8 145.8 %copy-start.51 = (f32[2048]{0:T(1024)S(1)}, f32[2048]{0:T(1024)}, u32[]{:S(2)}) copy-start(f32[2048]{0:T(1024)} %param.41) | copy-start | bytes 24580
  532.8 231.5 %all-gather.24.cloned.1.call-start = ((), (), s32[]{:S(2)}) async-start(), calls=%async_computation.19 | async-start | bytes 5242880 | tf_op jit(solution)/shard_map/all_gather | solution.py:248
  682.8 254.0 %reduce-scatter.15.cloned.1.call-start = ((), (), s32[]{:S(2)}) async-start(), calls=%async_computation.20 | async-start | bytes 10485760 | tf_op jit(solution)/shard_map/reduce_scatter | solution.py:263
  793.6 233.6 %all-gather.26.cloned.1.call-start = ((), (), s32[]{:S(2)}) async-start(), calls=%async_computation.21 | async-start | bytes 5242880 | tf_op jit(solution)/shard_map/all_gather | solution.py:269
  945.6 238.3 %reduce-scatter.27.cloned.1.call-start = ((), (), s32[]{:S(2)}) async-start(), calls=%async_computation.27 | async-start | bytes 9437184 | tf_op jit(solution)/shard_map/reduce_scatter | solution.py:256
  959.9 227.0 %reduce-scatter.29.cloned.1.call-start = ((), (), s32[]{:S(2)}) async-start(), calls=%async_computation.28 | async-start | bytes 9437184 | tf_op jit(solution)/shard_map/reduce_scatter | solution.py:259
  974.1 60.3 %copy-start.2 = (bf16[1024,8,64]{0,2,1:T(8,128)(2,1)S(1)}, bf16[1024,8,64]{0,2,1:T(8,128)(2,1)}, u32[]{:S(2)}) copy-start(bf16[1024,8,64]{0,2,1:T(8,128)(2,1)} %copy-done.1) | copy-start | bytes 3145732
  974.1 60.3 %copy-start.31 = (f32[8,128]{1,0:T(8,128)S(1)}, f32[8,128]{1,0:T(8,128)}, u32[]{:S(2)}) copy-start(f32[8,128]{1,0:T(8,128)} %copy-done.30) | copy-start | bytes 12292
  974.1 60.3 %copy-start.33 = (f32[2,8,512]{2,1,0:T(8,128)S(1)}, f32[2,8,512]{2,1,0:T(8,128)}, u32[]{:S(2)}) copy-start(f32[2,8,512]{2,1,0:T(8,128)} %copy-done.32) | copy-start | bytes 98308
  974.1 60.3 %copy-start.37 = (bf16[8,8]{1,0:T(8,128)(2,1)S(1)}, bf16[8,8]{1,0:T(8,128)(2,1)}, u32[]{:S(2)}) copy-start(bf16[8,8]{1,0:T(8,128)(2,1)} %copy-done.36) | copy-start | bytes 388
  974.1 60.3 %copy-start.54 = (s32[1024]{0:T(1024)S(1)}, s32[1024]{0:T(1024)}, u32[]{:S(2)}) copy-start(s32[1024]{0:T(1024)} %copy-done.53) | copy-start | bytes 12292
  974.1 60.3 %copy-start.63 = (s32[2]{0:T(128)S(1)}, s32[2]{0:T(128)}, u32[]{:S(2)}) copy-start(s32[2]{0:T(128)} %copy-done.62) | copy-start | bytes 28
  974.2 348.3 %reduce-scatter.17.cloned.1.call-start = ((), (), s32[]{:S(2)}) async-start(), calls=%async_computation.22 | async-start | bytes 10485760 | tf_op jit(solution)/shard_map/reduce_scatter | solution.py:293
  1039.9 9.8 copy-start.3
  1043.7 6.0 copy-start
  1068.0 12.6 copy-start.13
  1090.5 9.3 copy-start.3
  1121.1 12.8 copy-start.13
  1153.6 224.5 %reduce-scatter.25.cloned.1.call-start = ((), (), s32[]{:S(2)}) async-start(), calls=%async_computation.26 | async-start | bytes 4718592 | tf_op jit(solution)/shard_map/reduce_scatter | solution.py:286
  1161.5 271.6 %reduce-scatter.23.cloned.1.call-start = ((), (), s32[]{:S(2)}) async-start(), calls=%async_computation.25 | async-start | bytes 4718592 | tf_op jit(solution)/shard_map/reduce_scatter | solution.py:285
  1168.4 319.7 %reduce-scatter.21.cloned.1.call-start = ((), (), s32[]{:S(2)}) async-start(), calls=%async_computation.24 | async-start | bytes 4718592 | tf_op jit(solution)/shard_map/reduce_scatter | solution.py:284
  1176.2 366.9 %reduce-scatter.19.cloned.1.call-start = ((), (), s32[]{:S(2)}) async-start(), calls=%async_computation.23 | async-start | bytes 4718592 | tf_op jit(solution)/shard_map/reduce_scatter | solution.py:283
  1182.8 139.6 %copy-start.8 = (bf16[256,2048]{1,0:T(8,128)(2,1)S(1)}, bf16[256,2048]{1,0:T(8,128)(2,1)}, u32[]{:S(2)}) copy-start(bf16[256,2048]{1,0:T(8,128)(2,1)} %param.26) | copy-start | bytes 3145732
  1182.8 139.6 %copy-start.34 = (f32[2048]{0:T(1024)S(1)}, f32[2048]{0:T(1024)}, u32[]{:S(2)}) copy-start(f32[2048]{0:T(1024)} %param.27) | copy-start | bytes 24580
  1182.8 139.6 %copy-start.39 = (f32[256]{0:T(256)S(1)}, f32[256]{0:T(256)}, u32[]{:S(2)}) copy-start(f32[256]{0:T(256)} %copy-done.38) | copy-start | bytes 3076
  1186.9 137.8 %copy-start.47 = (f32[256]{0:T(256)S(1)}, f32[256]{0:T(256)}, u32[]{:S(2)}) copy-start(f32[256]{0:T(256)} %copy-done.46) | copy-start | bytes 3076
  1186.9 137.8 %copy-start.45 = (f32[256]{0:T(256)S(1)}, f32[256]{0:T(256)}, u32[]{:S(2)}) copy-start(f32[256]{0:T(256)} %copy-done.44) | copy-start | bytes 3076
  1189.7 136.0 %copy-start.40 = (f32[2048]{0:T(1024)S(1)}, f32[2048]{0:T(1024)}, u32[]{:S(2)}) copy-start(f32[2048]{0:T(1024)} %get-tuple-element.454) | copy-start | bytes 24580
  1189.7 136.0 %copy-start.41 = (f32[2048]{0:T(1024)S(1)}, f32[2048]{0:T(1024)}, u32[]{:S(2)}) copy-start(f32[2048]{0:T(1024)} %get-tuple-element.460) | copy-start | bytes 24580
  1189.7 136.0 %copy-start.42 = (f32[2048]{0:T(1024)S(1)}, f32[2048]{0:T(1024)}, u32[]{:S(2)}) copy-start(f32[2048]{0:T(1024)} %get-tuple-element.527) | copy-start | bytes 24580
  1189.7 136.0 %copy-start.43 = (f32[2048]{0:T(1024)S(1)}, f32[2048]{0:T(1024)}, u32[]{:S(2)}) copy-start(f32[2048]{0:T(1024)} %get-tuple-element.547) | copy-start | bytes 24580
  1189.7 181.7 %copy-start.11 = (f32[256,2048]{1,0:T(8,128)S(1)}, f32[256,2048]{1,0:T(8,128)}, u32[]{:S(2)}) copy-start(f32[256,2048]{1,0:T(8,128)} %copy-done.10) | copy-start | bytes 6291460
  (35 other events, 84.2 us)
Sparse Core Ops, SparseCore 0:
  9.9 30.5 all-gather.13
  42.7 80.7 all-gather.9
  125.3 26.2 all-gather.15
  153.4 27.7 all-gather.11
  182.9 27.7 all-gather.17
  233.1 144.6 reduce-scatter.10
  381.7 81.3 all-gather.19
  465.0 53.0 all-gather.21
  532.9 145.6 reduce-scatter.12
  682.9 81.2 all-gather.23
  793.7 143.0 reduce-scatter.14
  945.7 81.3 all-gather.25
  1030.6 69.9 reduce-scatter.26
  1103.9 71.5 reduce-scatter.28
  1177.7 144.6 reduce-scatter.16
  1326.2 51.8 reduce-scatter.24
  1381.9 51.1 reduce-scatter.22
  1436.9 51.1 reduce-scatter.20
  1492.0 51.1 reduce-scatter.18
